TPU v7x, 128 devices: a whole 4x4x4 slice. The times are simulated.
128 devices in a mesh: req: 32 (over z_hi, x, y), tp: 4 (over z_lo, core).
Axes of the slice: x: 4, y: 4, z: 4 (z_hi: 2, z_lo: 2; z = z_hi * 2 + z_lo), core: 2. Of those that a mesh axis runs over, the one named last changes fastest.
Arguments:
- hidden_in: bfloat16 [65536, 1024], P('req'), may hold values from -6 to 6
- lengths: int32 [64], replicated, may hold values from 1 to 2048, 65536 in all
- tenant: int32 [64], replicated, may hold values from 0 to 3
- shard_map: int32 [128], replicated, may hold values from 0 to 127, each once
- wq: float32 [1024, 1024], P(('req', 'tp')), as said below
- wk: float32 [1024, 1024], P(('req', 'tp')), as said below
- wv: float32 [1024, 1024], P(('req', 'tp')), may hold values from -0.75 to 0.75
- wo: float32 [1024, 1024], P(('req', 'tp')), may hold values from -0.75 to 0.75
- wi_in: float32 [1024, 2624], P(('req', 'tp')), may hold values from -0.1875 to 0.1875
- wi_gate: float32 [1024, 2624], P(('req', 'tp')), may hold values from -0.1875 to 0.1875
- wo2: float32 [1024, 2624], P(('req', 'tp')), may hold values from -0.125 to 0.125
- head: float32 [49152, 1024], P(('req', 'tp')), may hold values from -0.56 to 0.56
- attn_gain: float32 [1024], replicated, may hold values from 0.1 to 1.9
- mlp_gain: float32 [1024], replicated, may hold values from 0.1 to 1.9
- final_gain: float32 [4, 1024], replicated, may hold values from 0.1 to 1.9
Outputs:
- hidden_out: bfloat16 [65536, 1024], P('req', 'tp')
- cache: bfloat16 [2, 65536, 1024], P(None, 'req', 'tp')
- last_rms: float32 [64], replicated
- top_logit: float32 [64], replicated
Inputs may be any that keep to these rules, and one draw needn't show every extreme that they name: Prompts are packed in request order into the 65536 slots; the lengths sum to 65536 and the longest is exactly 2048. `shard_map`: A permutation: each row block is held by exactly one trainer device. `wq`: A fan-in scaled projection. `wk`: A fan-in scaled projection.
All inputs are finite; a program needn't handle non-finite values.
Results may differ from a plain program's by a relative error of at most 0.012.
The roundings to bfloat16 on the way count: a program that leaves them out, or rounds other values in their place, can miss the bound.
Values may be sent and summed in bfloat16 or wider, within the bound.
No kernel may reach another device: no remote copies, remote signals or barrier semaphores. Data moves between devices by JAX's collectives and lax.ppermute only.
A program may use at most 128 MiB of HBM per device.

v0:
```python
import jax
import jax.numpy as jnp
from jax import lax
from jax.sharding import PartitionSpec as P

HEADS = 16
HEAD_DIM = 64
THETA = 160000.0
EPS = 1e-05


def with_halo(block, sides, width):
    for axis, dim in sides:
        count = lax.axis_size(axis)
        forward = [(i, i + 1) for i in range(count - 1)]
        backward = [(target, source) for source, target in forward]
        low = lax.ppermute(
            lax.slice_in_dim(block, block.shape[dim] - width, None, axis=dim), axis, forward
        )
        high = lax.ppermute(lax.slice_in_dim(block, 0, width, axis=dim), axis, backward)
        block = jnp.concatenate([low, block, high], axis=dim)
    return block


def layer_norm(values, gain):
    center = jnp.mean(values, axis=-1, keepdims=True)
    spread = jnp.mean(values * values, axis=-1, keepdims=True) - center * center
    return (values - center) * lax.rsqrt(spread + EPS) * gain


def rotate(values, position):
    half = values.shape[-1] // 2
    freq = THETA ** (-(2.0 * jnp.arange(half, dtype=jnp.float32)) / values.shape[-1])
    angle = position.astype(jnp.float32)[:, None] * freq[None, :]
    cosine = jnp.cos(angle)[:, None, :]
    sine = jnp.sin(angle)[:, None, :]
    first = values[..., :half]
    second = values[..., half:]
    return jnp.concatenate(
        [first * cosine - second * sine, second * cosine + first * sine], axis=-1
    )


def reorder(weight, holder, shard_map, count):
    block_of = shard_map[holder]
    order = jnp.zeros((count,), jnp.int32).at[block_of].set(jnp.arange(count, dtype=jnp.int32))
    rows = weight.shape[0] // count
    return weight.reshape(count, rows, weight.shape[1])[order].reshape(
        weight.shape[0], weight.shape[1]
    )


def body(
    hidden_in,
    lengths,
    tenant,
    shard_map,
    wq,
    wk,
    wv,
    wo,
    wi_in,
    wi_gate,
    wo2,
    head,
    attn_gain,
    mlp_gain,
    final_gain,
):
    req_count = lax.axis_size("req")
    tp_count = lax.axis_size("tp")
    count = req_count * tp_count
    req_index = lax.axis_index("req")
    tp_index = lax.axis_index("tp")
    slots, width = hidden_in.shape
    local_heads = HEADS // tp_count
    share = width // tp_count
    served = (
        wq.astype(jnp.bfloat16),
        wk.astype(jnp.bfloat16),
        wv.astype(jnp.bfloat16),
        wo.astype(jnp.bfloat16),
        wi_in.astype(jnp.bfloat16),
        wi_gate.astype(jnp.bfloat16),
        wo2.astype(jnp.bfloat16),
    )
    place = jnp.arange(count, dtype=jnp.int32)
    collected = (
        lax.all_gather(served[0], "req", axis=0, tiled=True),
        lax.all_gather(served[1], "req", axis=0, tiled=True),
        lax.all_gather(served[2], "req", axis=0, tiled=True),
        lax.all_gather(served[3], "req", axis=0, tiled=True),
        lax.all_gather(served[4], "req", axis=0, tiled=True),
        lax.all_gather(served[5], "req", axis=0, tiled=True),
        lax.all_gather(served[6], "req", axis=0, tiled=True),
    )
    regrouped = (
        lax.all_to_all(collected[0], "tp", split_axis=1, concat_axis=0, tiled=True),
        lax.all_to_all(collected[1], "tp", split_axis=1, concat_axis=0, tiled=True),
        lax.all_to_all(collected[2], "tp", split_axis=1, concat_axis=0, tiled=True),
        lax.all_to_all(collected[3], "tp", split_axis=1, concat_axis=0, tiled=True),
        lax.all_to_all(collected[4], "tp", split_axis=1, concat_axis=0, tiled=True),
        lax.all_to_all(collected[5], "tp", split_axis=1, concat_axis=0, tiled=True),
        lax.all_to_all(collected[6], "tp", split_axis=1, concat_axis=0, tiled=True),
    )
    holder = place % req_count * tp_count + place // req_count
    query_w, key_w, value_w, out_w, input_w, gate_w, down_w = [
        reorder(item, holder, shard_map, count) for item in regrouped
    ]
    ends = jnp.cumsum(lengths)
    total = slots * req_count
    base = req_index * slots
    global_index = base - slots + jnp.arange(3 * slots, dtype=jnp.int32)
    before = ends[None, :] <= global_index[:, None]
    segment = jnp.sum(before.astype(jnp.int32), axis=1)
    inside = (global_index >= 0) & (global_index < total)
    segment = jnp.where(inside, segment, -1)
    own_segment = segment[slots : 2 * slots]
    own_index = global_index[slots : 2 * slots]
    own_before = before[slots : 2 * slots]
    position = own_index - jnp.sum(jnp.where(own_before, lengths[None, :], 0), axis=1)
    normed = layer_norm(hidden_in.astype(jnp.float32), attn_gain).astype(jnp.bfloat16)
    query = jnp.dot(normed, query_w, preferred_element_type=jnp.float32).reshape(
        slots, local_heads, HEAD_DIM
    )
    query = rotate(query, position).astype(jnp.bfloat16)
    keys = jnp.dot(normed, key_w, preferred_element_type=jnp.float32).reshape(
        slots, local_heads, HEAD_DIM
    )
    keys = rotate(keys, position).astype(jnp.bfloat16).reshape(slots, share)
    values = jnp.dot(normed, value_w, preferred_element_type=jnp.float32).astype(jnp.bfloat16)
    cache = jnp.stack([keys, values])
    widened = with_halo(cache, (("req", 1),), slots)
    key_heads = widened[0].reshape(3 * slots, local_heads, HEAD_DIM).transpose(1, 0, 2)
    value_heads = widened[1].reshape(3 * slots, local_heads, HEAD_DIM).transpose(1, 0, 2)
    query_heads = query.transpose(1, 0, 2)
    block = min(512, slots)
    scale = HEAD_DIM ** (-0.5)

    def head_attend(operands):
        query_head, key_head, value_head = operands

        def one_block(number):
            start = number * block
            query_block = lax.dynamic_slice_in_dim(query_head, start, block, 0)
            query_segment = lax.dynamic_slice_in_dim(own_segment, start, block, 0)
            scores = (
                lax.dot_general(
                    query_block,
                    key_head,
                    (((1,), (1,)), ((), ())),
                    preferred_element_type=jnp.float32,
                )
                * scale
            )
            scores = jnp.where(query_segment[:, None] == segment[None, :], scores, -1e30)
            highest = jnp.max(scores, axis=-1, keepdims=True)
            weights = jnp.exp(scores - highest)
            probability = (weights / jnp.sum(weights, axis=-1, keepdims=True)).astype(jnp.bfloat16)
            return jnp.dot(probability, value_head, preferred_element_type=jnp.float32)

        result = lax.map(one_block, jnp.arange(slots // block, dtype=jnp.int32))
        return result.reshape(slots, HEAD_DIM)

    attended = lax.map(head_attend, (query_heads, key_heads, value_heads))
    mixed = attended.transpose(1, 0, 2).reshape(slots, share).astype(jnp.bfloat16)
    attn_part = lax.dot_general(
        mixed, out_w, (((1,), (1,)), ((), ())), preferred_element_type=jnp.float32
    )
    summed = lax.psum(attn_part, "tp")
    first = (hidden_in.astype(jnp.float32) + summed).astype(jnp.bfloat16)
    normed2 = layer_norm(first.astype(jnp.float32), mlp_gain).astype(jnp.bfloat16)
    first_share = lax.dynamic_slice_in_dim(first, tp_index * share, share, 1)
    gate_in = jnp.dot(normed2, input_w, preferred_element_type=jnp.float32)
    gate_side = jnp.dot(normed2, gate_w, preferred_element_type=jnp.float32)
    inner = (jax.nn.gelu(gate_in, approximate=False) * gate_side).astype(jnp.bfloat16)
    down_part = lax.dot_general(
        inner, down_w, (((1,), (1,)), ((), ())), preferred_element_type=jnp.float32
    )
    down_share = lax.psum_scatter(down_part, "tp", scatter_dimension=1, tiled=True)
    hidden_out = (first_share.astype(jnp.float32) + down_share).astype(jnp.bfloat16)
    last_slot = ends - 1 - base
    holds = (last_slot >= 0) & (last_slot < slots)
    picked = hidden_out[jnp.clip(last_slot, 0, slots - 1)].astype(jnp.float32)
    picked = jnp.where(holds[:, None], picked, 0.0)
    request_count = lengths.shape[0]
    placed = lax.dynamic_update_slice(
        jnp.zeros((request_count, width), jnp.float32), picked, (jnp.int32(0), tp_index * share)
    )
    last = lax.psum(placed, ("req", "tp"))
    last_rms = jnp.sqrt(jnp.mean(last * last, axis=-1))
    choose = (tenant[:, None] == jnp.arange(final_gain.shape[0], dtype=jnp.int32)[None, :]).astype(
        jnp.float32
    )
    gain_rows = jnp.dot(
        choose, final_gain, precision=lax.Precision.HIGHEST, preferred_element_type=jnp.float32
    )
    final = layer_norm(last, gain_rows).astype(jnp.bfloat16)
    logits = lax.dot_general(
        final,
        head.astype(jnp.bfloat16),
        (((1,), (1,)), ((), ())),
        preferred_element_type=jnp.float32,
    )
    top_logit = lax.pmax(jnp.max(logits, axis=-1), ("req", "tp"))
    return (hidden_out, cache, last_rms, top_logit)


def solution(mesh):
    placed = (
        P("req", None),
        P(),
        P(),
        P(),
        P(("req", "tp"), None),
        P(("req", "tp"), None),
        P(("req", "tp"), None),
        P(("req", "tp"), None),
        P(("req", "tp"), None),
        P(("req", "tp"), None),
        P(("req", "tp"), None),
        P(("req", "tp"), None),
        P(),
        P(),
        P(),
    )
    return jax.shard_map(
        body,
        mesh=mesh,
        in_specs=placed,
        out_specs=(P("req", "tp"), P(None, "req", "tp"), P(), P()),
        check_vma=False,
    )
```

profile of v0, /device:TPU:1, one launch (start us, length us, event | category | flops | bytes accessed | tf_op | source)
XLA Modules:
  0.0 1209.6 jit_solution(8971452301709203540)
XLA Ops:
  10.4 85.3 %all_gather.22 = bf16[256,1024]{1,0:T(8,128)(2,1)S(1)} all-gather(bf16[8,1024]{1,0:T(8,128)(2,1)S(1)} %convert_element_type.94), channel_id=1, replica_groups=mesh['req'=32,'tp'=4] {'req'}, dimensions={0}, use_global_device_ids=true | all-gather | bytes 540672 | tf_op jit(solution)/shard_map/all_gather | solution.py:90
  96.7 18.5 %all-to-all-start.1 = ((bf16[256,4,256]{0,2,1:T(8,128)(2,1)}), bf16[256,4,256]{0,2,1:T(8,128)(2,1)S(1)}, u32[]{:S(2)}, u32[]{:S(2)}) async-start(bf16[256,4,256]{0,2,1:T(8,128)(2,1)} %bitcast.18), calls=%async_computation.1 | async-start | bytes 1048576 | tf_op jit(solution)/shard_map/all_to_all | solution.py:99
  124.0 76.5 %all_gather.21 = bf16[256,1024]{1,0:T(8,128)(2,1)S(1)} all-gather(bf16[8,1024]{1,0:T(8,128)(2,1)S(1)} %convert_element_type.92), channel_id=1, replica_groups=mesh['req'=32,'tp'=4] {'req'}, dimensions={0}, use_global_device_ids=true | all-gather | bytes 540672 | tf_op jit(solution)/shard_map/all_gather | solution.py:89
  200.5 78.2 %all_gather.23 = bf16[256,1024]{1,0:T(8,128)(2,1)S(1)} all-gather(bf16[8,1024]{1,0:T(8,128)(2,1)S(1)} %convert_element_type.96), channel_id=1, replica_groups=mesh['req'=32,'tp'=4] {'req'}, dimensions={0}, use_global_device_ids=true | all-gather | bytes 540672 | tf_op jit(solution)/shard_map/all_gather | solution.py:91
  279.0 4.3 fusion.12
  285.6 31.4 %all-to-all-start = ((bf16[256,4,256]{0,2,1:T(8,128)(2,1)}), bf16[256,4,256]{0,2,1:T(8,128)(2,1)S(1)}, u32[]{:S(2)}, u32[]{:S(2)}) async-start(bf16[256,4,256]{0,2,1:T(8,128)(2,1)} %bitcast.7), calls=%async_computation | async-start | bytes 1048576 | tf_op jit(solution)/shard_map/all_to_all | solution.py:98
  319.0 5.9 all-to-all-done
  325.0 4.8 all-to-all-start.2
  330.8 3.7 fusion.26
  347.1 114.9 %all_gather.24 = bf16[256,1024]{1,0:T(8,128)(2,1)S(1)} all-gather(bf16[8,1024]{1,0:T(8,128)(2,1)S(1)} %convert_element_type.102), channel_id=1, replica_groups=mesh['req'=32,'tp'=4] {'req'}, dimensions={0}, use_global_device_ids=true | all-gather | bytes 540672 | tf_op jit(solution)/shard_map/all_gather | solution.py:92
  463.0 17.3 %all-to-all-start.3 = ((bf16[256,4,256]{0,2,1:T(8,128)(2,1)}), bf16[256,4,256]{0,2,1:T(8,128)(2,1)S(1)}, u32[]{:S(2)}, u32[]{:S(2)}) async-start(bf16[256,4,256]{0,2,1:T(8,128)(2,1)} %bitcast.36), calls=%async_computation.3 | async-start | bytes 1048576 | tf_op jit(solution)/shard_map/all_to_all | solution.py:101
  481.6 6.9 all-to-all-done.3
  496.5 4.8 copy.103
  504.5 160.4 %while.21 = (s32[]{:T(128)}, bf16[4,2048,64]{1,2,0:T(8,128)(2,1)}, bf16[4,2048,64]{1,2,0:T(8,128)(2,1)}, bf16[4,6144,64]{1,2,0:T(8,128)(2,1)}, bf16[4,6144,64]{1...) while((s32[]{:T(128)}, bf16[4,2048,64]{1,2,0:T(8,128)(2,1)}, ...), condition=%wide.region_11.12_spmd, body=%wide.region_6.0_spmd.sunk | while | flops 833616896 | bytes 53257172 | solution.py:165
  509.6 33.7 %while.22 = (s32[]{:T(128)}, bf16[4,512,64]{1,2,0:T(8,128)(2,1)S(1)}, s32[4]{0:T(128)S(1)}, s32[2048]{0:T(1024)S(1)}, s32[6144]{0:T(1024)S(1)}, /*index=5*/bf16[...) while((s32[]{:T(128)}, ...), condition=%wide.region_10.10_spmd, body=%wide.region_7.9_spmd.sunk | while | flops 833616896 | bytes 44343512 | solution.py:162
  549.7 33.7 %while.22 = (s32[]{:T(128)}, bf16[4,512,64]{1,2,0:T(8,128)(2,1)S(1)}, s32[4]{0:T(128)S(1)}, s32[2048]{0:T(1024)S(1)}, s32[6144]{0:T(1024)S(1)}, /*index=5*/bf16[...) while((s32[]{:T(128)}, ...), condition=%wide.region_10.10_spmd, body=%wide.region_7.9_spmd.sunk | while | flops 833616896 | bytes 44343512 | solution.py:162
  589.8 33.7 %while.22 = (s32[]{:T(128)}, bf16[4,512,64]{1,2,0:T(8,128)(2,1)S(1)}, s32[4]{0:T(128)S(1)}, s32[2048]{0:T(1024)S(1)}, s32[6144]{0:T(1024)S(1)}, /*index=5*/bf16[...) while((s32[]{:T(128)}, ...), condition=%wide.region_10.10_spmd, body=%wide.region_7.9_spmd.sunk | while | flops 833616896 | bytes 44343512 | solution.py:162
  629.9 33.7 %while.22 = (s32[]{:T(128)}, bf16[4,512,64]{1,2,0:T(8,128)(2,1)S(1)}, s32[4]{0:T(128)S(1)}, s32[2048]{0:T(1024)S(1)}, s32[6144]{0:T(1024)S(1)}, /*index=5*/bf16[...) while((s32[]{:T(128)}, ...), condition=%wide.region_10.10_spmd, body=%wide.region_7.9_spmd.sunk | while | flops 833616896 | bytes 44343512 | solution.py:162
  664.8 5.9 fusion.69
  673.3 4.4 all-to-all-start.4
  680.2 21.4 %all-to-all-done.4 = bf16[256,4,656]{0,2,1:T(8,128)(2,1)S(1)} async-done(((bf16[256,4,656]{0,2,1:T(8,128)(2,1)}), bf16[256,4,656]{0,2,1:T(8,128)(2,1)S(1)}, u32[]{:S(2)}, u32[]{:S(2)}) %all-to-all-start.4) | async-done | bytes 1343520 | tf_op jit(solution)/shard_map/all_to_all | solution.py:102
  701.6 5.2 all-to-all-start.5
  709.3 29.3 %all-to-all-done.5 = bf16[256,4,656]{0,2,1:T(8,128)(2,1)S(1)} async-done(((bf16[256,4,656]{0,2,1:T(8,128)(2,1)}), bf16[256,4,656]{0,2,1:T(8,128)(2,1)S(1)}, u32[]{:S(2)}, u32[]{:S(2)}) %all-to-all-start.5) | async-done | bytes 1343520 | tf_op jit(solution)/shard_map/all_to_all | solution.py:103
  738.6 5.0 all-to-all-start.6
  748.8 26.2 %all-to-all-done.6 = bf16[256,4,656]{0,2,1:T(8,128)(2,1)} async-done(((bf16[256,4,656]{0,2,1:T(8,128)(2,1)}), bf16[256,4,656]{0,2,1:T(8,128)(2,1)}, u32[]{:S(2)}, u32[]{:S(2)}) %all-to-all-start.6) | async-done | bytes 1343520 | tf_op jit(solution)/shard_map/all_to_all | solution.py:104
  778.7 95.2 %all-reduce.3.cloned.1.call-done = f32[2048,1024]{1,0:T(8,128)} async-done(((f32[2048,1024]{1,0:T(8,128)}), f32[2048,1024]{1,0:T(8,128)}) %all-reduce.3.cloned.1.call-update) | async-done | bytes 8388624 | tf_op jit(solution)/shard_map/psum | solution.py:170
  873.8 5.5 convert_reduce_fusion.1
  881.3 5.4 fusion.65
  886.7 23.0 %fusion.30 = f32[2048,1024]{1,0:T(8,128)} fusion(f32[2048,656]{0,1:T(8,128)} %fusion.65, bf16[128,8,656]{2,1,0:T(8,128)(2,1)} %gather_fusion.7, bf16[128,8,656]{2,1,0:T(8,128)(2,1)S(1)} %copy-done.12, bf16[2048,1024]{1,0:T(8,128)(2,1)} %copy-done.5, f32[1024]{0:T(1024)S(1)} %copy-done.25, f32[2048]{0:T(1024)S(1)} %get-tuple-element.173, ...), kind=kOutput, calls=%fused_computation.64 | convolution fusion | flops 5602082816 | bytes 20664320 | tf_op jit(solution)/shard_map/dot_general | solution.py:177
  910.4 79.1 %reduce-scatter.2.cloned.1.call-done = f32[2048,256]{1,0:T(8,128)} async-done(((f32[2048,1024]{1,0:T(8,128)}), f32[2048,256]{1,0:T(8,128)}) %reduce-scatter.2.cloned.1.call-update) | async-done | bytes 2097168 | tf_op jit(solution)/shard_map/reduce_scatter | solution.py:180
  993.2 142.3 %all-reduce.5.cloned.1.call-done = f32[64,1024]{1,0:T(8,128)} async-done(((f32[64,1024]{1,0:T(8,128)}), f32[64,1024]{1,0:T(8,128)}) %all-reduce.5.cloned.1.call-update) | async-done | bytes 262160 | tf_op jit(solution)/shard_map/psum | solution.py:190
  1138.9 63.4 %pmax.7 = f32[64]{0:T(128)} all-reduce(f32[64]{0:T(128)S(1)} %convolution_reduce_fusion), channel_id=1, replica_groups=mesh['req'=32,'tp'=4] {'req','tp'}, use_global_device_ids=true, to_apply=%region_20.21 | all-reduce | flops 64 | bytes 512 | tf_op jit(solution)/shard_map/pmax | solution.py:205
  (296 shorter events, 218.9 us)
Async XLA Ops:
  8.0 1129.1 %copy-start = (f32[4,1024]{1,0:T(4,128)S(1)}, f32[4,1024]{1,0:T(4,128)}, u32[]{:S(2)}) copy-start(f32[4,1024]{1,0:T(4,128)} %param.33) | copy-start | bytes 49156
  8.0 113.7 %copy-start.1 = (s32[128]{0:T(128)S(1)}, s32[128]{0:T(128)}, u32[]{:S(2)}) copy-start(s32[128]{0:T(128)} %param.22) | copy-start | bytes 1540
  8.0 115.9 %copy-start.15 = (f32[8,1024]{1,0:T(8,128)S(1)}, f32[8,1024]{1,0:T(8,128)}, u32[]{:S(2)}) copy-start(f32[8,1024]{1,0:T(8,128)} %param.23) | copy-start | bytes 98308
  8.0 192.4 %copy-start.16 = (f32[8,1024]{1,0:T(8,128)S(1)}, f32[8,1024]{1,0:T(8,128)}, u32[]{:S(2)}) copy-start(f32[8,1024]{1,0:T(8,128)} %param.25) | copy-start | bytes 98308
  8.0 271.0 %copy-start.21 = (f32[1024]{0:T(1024)S(1)}, f32[1024]{0:T(1024)}, u32[]{:S(2)}) copy-start(f32[1024]{0:T(1024)} %param.31) | copy-start | bytes 12292
  8.1 662.7 %all-gather.4.cloned.1.call-start = ((), (), s32[]{:S(2)}) async-start(), calls=%async_computation.9 | async-start | bytes 1419264 | tf_op jit(solution)/shard_map/all_gather | solution.py:93
  96.7 188.8 %all-to-all-start.1 = ((bf16[256,4,256]{0,2,1:T(8,128)(2,1)}), bf16[256,4,256]{0,2,1:T(8,128)(2,1)S(1)}, u32[]{:S(2)}, u32[]{:S(2)}) async-start(bf16[256,4,256]{0,2,1:T(8,128)(2,1)} %bitcast.18), calls=%async_computation.1 | async-start | bytes 1048576 | tf_op jit(solution)/shard_map/all_to_all | solution.py:99
  115.2 562.5 %all-gather.6.cloned.1.call-start = ((), (), s32[]{:S(2)}) async-start(), calls=%async_computation.10 | async-start | bytes 1419264 | tf_op jit(solution)/shard_map/all_gather | solution.py:94
  118.2 363.1 %copy-start.19 = (s32[64]{0:T(128)}, s32[64]{0:T(128)S(1)}, u32[]{:S(2)}) copy-start(s32[64]{0:T(128)S(1)} %get-tuple-element.126) | copy-start | bytes 772
  124.0 364.7 %copy-start.18 = (s32[1024]{0:T(1024)}, s32[1024]{0:T(1024)S(1)}, u32[]{:S(2)}) copy-start(s32[1024]{0:T(1024)S(1)} %pad_clamp_fusion.1) | copy-start | bytes 12292
  279.0 6.4 copy-start.22
  285.6 39.4 %all-to-all-start = ((bf16[256,4,256]{0,2,1:T(8,128)(2,1)}), bf16[256,4,256]{0,2,1:T(8,128)(2,1)S(1)}, u32[]{:S(2)}, u32[]{:S(2)}) async-start(bf16[256,4,256]{0,2,1:T(8,128)(2,1)} %bitcast.7), calls=%async_computation | async-start | bytes 1048576 | tf_op jit(solution)/shard_map/all_to_all | solution.py:98
  325.0 13.3 %all-to-all-start.2 = ((bf16[256,4,256]{0,2,1:T(8,128)(2,1)}), bf16[256,4,256]{0,2,1:T(8,128)(2,1)S(1)}, u32[]{:S(2)}, u32[]{:S(2)}) async-start(bf16[256,4,256]{0,2,1:T(8,128)(2,1)} %bitcast.25), calls=%async_computation.2 | async-start | bytes 1048576 | tf_op jit(solution)/shard_map/all_to_all | solution.py:100
  339.1 7.9 copy-start.17
  342.6 137.7 %copy-start.14 = (f32[8,2624]{1,0:T(8,128)S(1)}, f32[8,2624]{1,0:T(8,128)}, u32[]{:S(2)}) copy-start(f32[8,2624]{1,0:T(8,128)} %param.29) | copy-start | bytes 251908
  342.8 147.3 %copy-start.9 = (bf16[2,2048,256]{2,1,0:T(8,128)(2,1)}, bf16[2,2048,256]{2,1,0:T(8,128)(2,1)S(1)}, u32[]{:S(2)}) copy-start(bf16[2,2048,256]{2,1,0:T(8,128)(2,1)S(1)} %pad_maximum_fusion.1) | copy-start | bytes 6291460
  342.8 147.3 %collective-permute-start = (bf16[2,2048,256]{2,1,0:T(8,128)(2,1)S(1)}, bf16[2,2048,256]{2,1,0:T(8,128)(2,1)}, u32[]{:S(2)}, u32[]{:S(2)}) collective-permute-start(bf16[2,2048,256]{2,1,0:T(8,128)(2,1)S(1)} %pad_maximum_fusion.1), channel_id=1, source_target_pairs={{0,4},{4,8},{8,12},{12,16},{16,20},{20,24},{24,28},{28,32},{32,36}... | collective-permute-start | bytes 6291464 | tf_op jit(solution)/shard_map/ppermute | solution.py:17
  345.7 144.4 %collective-permute-start.1 = (bf16[2,2048,256]{2,1,0:T(8,128)(2,1)S(1)}, bf16[2,2048,256]{2,1,0:T(8,128)(2,1)}, u32[]{:S(2)}, u32[]{:S(2)}) collective-permute-start(bf16[2,2048,256]{2,1,0:T(8,128)(2,1)S(1)} %pad_maximum_fusion.1), channel_id=1, source_target_pairs={{4,0},{8,4},{12,8},{16,12},{20,16},{24,20},{28,24},{32,28},{36,32}... | collective-permute-start | bytes 6291464 | tf_op jit(solution)/shard_map/ppermute | solution.py:20
  463.0 25.5 %all-to-all-start.3 = ((bf16[256,4,256]{0,2,1:T(8,128)(2,1)}), bf16[256,4,256]{0,2,1:T(8,128)(2,1)S(1)}, u32[]{:S(2)}, u32[]{:S(2)}) async-start(bf16[256,4,256]{0,2,1:T(8,128)(2,1)} %bitcast.36), calls=%async_computation.3 | async-start | bytes 1048576 | tf_op jit(solution)/shard_map/all_to_all | solution.py:101
  480.3 226.5 %all-gather.8.cloned.1.call-start = ((), (), s32[]{:S(2)}) async-start(), calls=%async_computation.11 | async-start | bytes 1419264 | tf_op jit(solution)/shard_map/all_gather | solution.py:95
  481.0 392.8 %all-reduce.3.cloned.1.call-start = ((), (), s32[]{:S(2)}) async-start(), calls=%async_computation.8 | async-start | bytes 16777216 | tf_op jit(solution)/shard_map/psum | solution.py:170
  673.3 28.3 %all-to-all-start.4 = ((bf16[256,4,656]{0,2,1:T(8,128)(2,1)}), bf16[256,4,656]{0,2,1:T(8,128)(2,1)S(1)}, u32[]{:S(2)}, u32[]{:S(2)}) async-start(bf16[256,4,656]{0,2,1:T(8,128)(2,1)} %bitcast.40), calls=%async_computation.4 | async-start | bytes 2686976 | tf_op jit(solution)/shard_map/all_to_all | solution.py:102
  701.6 37.0 %all-to-all-start.5 = ((bf16[256,4,656]{0,2,1:T(8,128)(2,1)}), bf16[256,4,656]{0,2,1:T(8,128)(2,1)S(1)}, u32[]{:S(2)}, u32[]{:S(2)}) async-start(bf16[256,4,656]{0,2,1:T(8,128)(2,1)} %bitcast.116), calls=%async_computation.5 | async-start | bytes 2686976 | tf_op jit(solution)/shard_map/all_to_all | solution.py:103
  738.6 5.2 copy-start.6
  738.6 36.5 %all-to-all-start.6 = ((bf16[256,4,656]{0,2,1:T(8,128)(2,1)}), bf16[256,4,656]{0,2,1:T(8,128)(2,1)}, u32[]{:S(2)}, u32[]{:S(2)}) async-start(bf16[256,4,656]{0,2,1:T(8,128)(2,1)} %bitcast.115), calls=%async_computation.6 | async-start | bytes 2686976 | tf_op jit(solution)/shard_map/all_to_all | solution.py:104
  743.5 246.0 %reduce-scatter.2.cloned.1.call-start = ((), (), s32[]{:S(2)}) async-start(), calls=%async_computation.12 | async-start | bytes 10485760 | tf_op jit(solution)/shard_map/reduce_scatter | solution.py:180
  778.7 102.7 %copy-start.25 = (f32[1024]{0:T(1024)S(1)}, f32[1024]{0:T(1024)}, u32[]{:S(2)}) copy-start(f32[1024]{0:T(1024)} %param.32) | copy-start | bytes 12292
  881.3 5.4 copy-start.12
  909.7 227.4 %copy-start.24 = (s32[64]{0:T(128)S(1)}, s32[64]{0:T(128)}, u32[]{:S(2)}) copy-start(s32[64]{0:T(128)} %param.21) | copy-start | bytes 772
  909.8 228.7 %copy-start.11 = (f32[384,1024]{1,0:T(8,128)S(1)}, f32[384,1024]{1,0:T(8,128)}, u32[]{:S(2)}) copy-start(f32[384,1024]{1,0:T(8,128)} %param.30) | copy-start | bytes 4718596
  909.8 225.7 %all-reduce.5.cloned.1.call-start = ((), (), s32[]{:S(2)}) async-start(), calls=%async_computation.13 | async-start | bytes 524288 | tf_op jit(solution)/shard_map/psum | solution.py:190
  991.7 210.6 %copy-start.10 = (bf16[2048,256]{1,0:T(8,128)(2,1)}, bf16[2048,256]{1,0:T(8,128)(2,1)S(1)}, u32[]{:S(2)}) copy-start(bf16[2048,256]{1,0:T(8,128)(2,1)S(1)} %add_convert_fusion) | copy-start | bytes 3145732
  (24 other events, 50.6 us)
Sparse Core Ops, SparseCore 0:
  12.0 70.7 all-gather.3
  119.1 62.6 all-gather.5
  484.2 72.7 all-gather.7
  993.3 142.1 all-reduce.4
Sparse Core Ops, SparseCore 1:
  670.8 202.9 all-reduce.2
  909.9 79.6 reduce-scatter.1
where the time goes:
time: 1220 us; the launch traced here: 1210 us
  blocking collectives  418 us (34%)
  waiting for transfers between devices  406 us (33%)
  matrix products  127 us (10%)
  starting transfers between devices  91.3 us (7%)
  local copies, waits for them, and re-layouts  80.1 us (7%)
  other arithmetic  59.5 us (5%)
  between operations  16 us (1%)
    psum x1, waiting for transfers between devices, body(): last = lax.psum(placed, ('req', 'tp'))  142 us
    all_gather x1, blocking collectives, body(): lax.all_gather(served[3], 'req', axis=0, tiled=True)  115 us
    psum x1, waiting for transfers between devices, body(): summed = lax.psum(attn_part, 'tp')  95.2 us
    all_gather x1, blocking collectives, body(): lax.all_gather(served[1], 'req', axis=0, tiled=True)  85.3 us
    reduce_scatter x1, waiting for transfers between devices, body(): lax.psum_scatter(down_part, 'tp', scatter_dimension=1, tiled=True)  79.1 us
    all_gather x1, blocking collectives, body(): lax.all_gather(served[2], 'req', axis=0, tiled=True)  78.2 us
    all_gather x1, blocking collectives, body(): lax.all_gather(served[0], 'req', axis=0, tiled=True)  76.5 us
    pmax x1, blocking collectives, body(): top_logit = lax.pmax(jnp.max(logits, axis=-1), ('req', 'tp'))  63.4 us
  transfers between devices with their start and end apart: 15, of which 8 were waited for; matrix products, arithmetic and copies ran while one was open for 18% of the time, Pallas kernels for 0%

commit v1 on v0

--- a/solution.py
+++ b/solution.py
@@ -167,7 +167,7 @@
     attn_part = lax.dot_general(
         mixed, out_w, (((1,), (1,)), ((), ())), preferred_element_type=jnp.float32
     )
-    summed = lax.psum(attn_part, "tp")
+    summed = jnp.sum(lax.all_gather(attn_part, "tp"), axis=0)
     first = (hidden_in.astype(jnp.float32) + summed).astype(jnp.bfloat16)
     normed2 = layer_norm(first.astype(jnp.float32), mlp_gain).astype(jnp.bfloat16)
     first_share = lax.dynamic_slice_in_dim(first, tp_index * share, share, 1)

time: 1220 us -> 1360 us (1.11)
  waiting for transfers between devices: 406 us -> 532 us
  other arithmetic: 59.5 us -> 76 us
    all_gather x0 -> x1, waiting for transfers between devices: none -> 226 us  [body(): summed = jnp.sum(lax.all_gather(attn_part, 'tp'), axis=0)]
    psum x1 -> x0, waiting for transfers between devices: 95.2 us -> none  [body(): summed = lax.psum(attn_part, 'tp')]
    reduce_sum x0 -> x1, other arithmetic: none -> 16.5 us  [body(): summed = jnp.sum(lax.all_gather(attn_part, 'tp'), axis=0)]
  transfers between devices with their start and end apart: 15 -> 15, of which waited for: 8 -> 8; matrix products, arithmetic and copies ran while one was open for 18% -> 16% of each run, Pallas kernels for 0% -> 0%
where the time goes in v1:
time: 1360 us; the launch traced here: 1350 us
  waiting for transfers between devices  532 us (39%)
  blocking collectives  419 us (31%)
  matrix products  127 us (9%)
  starting transfers between devices  90.9 us (7%)
  local copies, waits for them, and re-layouts  80.1 us (6%)
  other arithmetic  76 us (6%)
  between operations  14.9 us (1%)
    all_gather x1, waiting for transfers between devices, body(): summed = jnp.sum(lax.all_gather(attn_part, 'tp'), axis=0)  226 us
    psum x1, waiting for transfers between devices, body(): last = lax.psum(placed, ('req', 'tp'))  143 us
    all_gather x1, blocking collectives, body(): lax.all_gather(served[3], 'req', axis=0, tiled=True)  115 us
    all_gather x1, blocking collectives, body(): lax.all_gather(served[1], 'req', axis=0, tiled=True)  85.3 us
    reduce_scatter x1, waiting for transfers between devices, body(): lax.psum_scatter(down_part, 'tp', scatter_dimension=1, tiled=True)  80.5 us
    all_gather x1, blocking collectives, body(): lax.all_gather(served[2], 'req', axis=0, tiled=True)  78.2 us
    all_gather x1, blocking collectives, body(): lax.all_gather(served[0], 'req', axis=0, tiled=True)  76.6 us
    pmax x1, blocking collectives, body(): top_logit = lax.pmax(jnp.max(logits, axis=-1), ('req', 'tp'))  63.4 us
  transfers between devices with their start and end apart: 15, of which 8 were waited for; matrix products, arithmetic and copies ran while one was open for 16% of the time, Pallas kernels for 0%

profile of v1, /device:TPU:1, one launch (start us, length us, event | category | flops | bytes accessed | tf_op | source)
XLA Modules:
  0.0 1349.7 jit_solution(18030433842945099375)
XLA Ops:
  9.6 85.3 %all_gather.28 = bf16[256,1024]{1,0:T(8,128)(2,1)S(1)} all-gather(bf16[8,1024]{1,0:T(8,128)(2,1)S(1)} %convert_element_type.94), channel_id=1, replica_groups=mesh['req'=32,'tp'=4] {'req'}, dimensions={0}, use_global_device_ids=true | all-gather | bytes 540672 | tf_op jit(solution)/shard_map/all_gather | solution.py:90
  95.9 18.5 %all-to-all-start.1 = ((bf16[256,4,256]{0,2,1:T(8,128)(2,1)}), bf16[256,4,256]{0,2,1:T(8,128)(2,1)S(1)}, u32[]{:S(2)}, u32[]{:S(2)}) async-start(bf16[256,4,256]{0,2,1:T(8,128)(2,1)} %bitcast.18), calls=%async_computation.1 | async-start | bytes 1048576 | tf_op jit(solution)/shard_map/all_to_all | solution.py:99
  123.2 76.6 %all_gather.27 = bf16[256,1024]{1,0:T(8,128)(2,1)S(1)} all-gather(bf16[8,1024]{1,0:T(8,128)(2,1)S(1)} %convert_element_type.92), channel_id=1, replica_groups=mesh['req'=32,'tp'=4] {'req'}, dimensions={0}, use_global_device_ids=true | all-gather | bytes 540672 | tf_op jit(solution)/shard_map/all_gather | solution.py:89
  199.8 78.2 %all_gather.29 = bf16[256,1024]{1,0:T(8,128)(2,1)S(1)} all-gather(bf16[8,1024]{1,0:T(8,128)(2,1)S(1)} %convert_element_type.96), channel_id=1, replica_groups=mesh['req'=32,'tp'=4] {'req'}, dimensions={0}, use_global_device_ids=true | all-gather | bytes 540672 | tf_op jit(solution)/shard_map/all_gather | solution.py:91
  278.3 4.3 fusion.12
  284.9 31.4 %all-to-all-start = ((bf16[256,4,256]{0,2,1:T(8,128)(2,1)}), bf16[256,4,256]{0,2,1:T(8,128)(2,1)S(1)}, u32[]{:S(2)}, u32[]{:S(2)}) async-start(bf16[256,4,256]{0,2,1:T(8,128)(2,1)} %bitcast.7), calls=%async_computation | async-start | bytes 1048576 | tf_op jit(solution)/shard_map/all_to_all | solution.py:98
  318.4 5.9 all-to-all-done
  324.3 4.8 all-to-all-start.2
  346.5 114.9 %all_gather.30 = bf16[256,1024]{1,0:T(8,128)(2,1)S(1)} all-gather(bf16[8,1024]{1,0:T(8,128)(2,1)S(1)} %convert_element_type.102), channel_id=1, replica_groups=mesh['req'=32,'tp'=4] {'req'}, dimensions={0}, use_global_device_ids=true | all-gather | bytes 540672 | tf_op jit(solution)/shard_map/all_gather | solution.py:92
  462.4 17.3 %all-to-all-start.3 = ((bf16[256,4,256]{0,2,1:T(8,128)(2,1)}), bf16[256,4,256]{0,2,1:T(8,128)(2,1)S(1)}, u32[]{:S(2)}, u32[]{:S(2)}) async-start(bf16[256,4,256]{0,2,1:T(8,128)(2,1)} %bitcast.36), calls=%async_computation.3 | async-start | bytes 1048576 | tf_op jit(solution)/shard_map/all_to_all | solution.py:101
  481.0 6.9 all-to-all-done.3
  495.9 4.8 copy.103
  503.9 159.8 %while.21 = (s32[]{:T(128)}, bf16[4,2048,64]{1,2,0:T(8,128)(2,1)}, bf16[4,2048,64]{1,2,0:T(8,128)(2,1)}, bf16[4,6144,64]{1,2,0:T(8,128)(2,1)}, bf16[4,6144,64]{1...) while((s32[]{:T(128)}, bf16[4,2048,64]{1,2,0:T(8,128)(2,1)}, ...), condition=%wide.region_11.12_spmd, body=%wide.region_6.0_spmd.sunk | while | flops 833616896 | bytes 53257172 | solution.py:165
  509.0 33.6 %while.22 = (s32[]{:T(128)}, bf16[4,512,64]{1,2,0:T(8,128)(2,1)S(1)}, s32[4]{0:T(128)S(1)}, s32[2048]{0:T(1024)S(1)}, s32[6144]{0:T(1024)S(1)}, /*index=5*/bf16[...) while((s32[]{:T(128)}, ...), condition=%wide.region_10.10_spmd, body=%wide.region_7.9_spmd.sunk | while | flops 833616896 | bytes 44343512 | solution.py:162
  548.9 33.6 %while.22 = (s32[]{:T(128)}, bf16[4,512,64]{1,2,0:T(8,128)(2,1)S(1)}, s32[4]{0:T(128)S(1)}, s32[2048]{0:T(1024)S(1)}, s32[6144]{0:T(1024)S(1)}, /*index=5*/bf16[...) while((s32[]{:T(128)}, ...), condition=%wide.region_10.10_spmd, body=%wide.region_7.9_spmd.sunk | while | flops 833616896 | bytes 44343512 | solution.py:162
  588.9 33.6 %while.22 = (s32[]{:T(128)}, bf16[4,512,64]{1,2,0:T(8,128)(2,1)S(1)}, s32[4]{0:T(128)S(1)}, s32[2048]{0:T(1024)S(1)}, s32[6144]{0:T(1024)S(1)}, /*index=5*/bf16[...) while((s32[]{:T(128)}, ...), condition=%wide.region_10.10_spmd, body=%wide.region_7.9_spmd.sunk | while | flops 833616896 | bytes 44343512 | solution.py:162
  628.8 33.6 %while.22 = (s32[]{:T(128)}, bf16[4,512,64]{1,2,0:T(8,128)(2,1)S(1)}, s32[4]{0:T(128)S(1)}, s32[2048]{0:T(1024)S(1)}, s32[6144]{0:T(1024)S(1)}, /*index=5*/bf16[...) while((s32[]{:T(128)}, ...), condition=%wide.region_10.10_spmd, body=%wide.region_7.9_spmd.sunk | while | flops 833616896 | bytes 44343512 | solution.py:162
  663.6 5.9 fusion.69
  672.1 4.4 all-to-all-start.4
  679.0 14.2 %all-to-all-done.4 = bf16[256,4,656]{0,2,1:T(8,128)(2,1)S(1)} async-done(((bf16[256,4,656]{0,2,1:T(8,128)(2,1)}), bf16[256,4,656]{0,2,1:T(8,128)(2,1)S(1)}, u32[]{:S(2)}, u32[]{:S(2)}) %all-to-all-start.4) | async-done | bytes 1343520 | tf_op jit(solution)/shard_map/all_to_all | solution.py:102
  693.2 4.5 all-to-all-start.5
  700.6 28.4 %all-to-all-done.5 = bf16[256,4,656]{0,2,1:T(8,128)(2,1)S(1)} async-done(((bf16[256,4,656]{0,2,1:T(8,128)(2,1)}), bf16[256,4,656]{0,2,1:T(8,128)(2,1)S(1)}, u32[]{:S(2)}, u32[]{:S(2)}) %all-to-all-start.5) | async-done | bytes 1343520 | tf_op jit(solution)/shard_map/all_to_all | solution.py:103
  729.0 5.2 all-to-all-start.6
  739.5 26.2 %all-to-all-done.6 = bf16[256,4,656]{0,2,1:T(8,128)(2,1)} async-done(((bf16[256,4,656]{0,2,1:T(8,128)(2,1)}), bf16[256,4,656]{0,2,1:T(8,128)(2,1)}, u32[]{:S(2)}, u32[]{:S(2)}) %all-to-all-start.6) | async-done | bytes 1343520 | tf_op jit(solution)/shard_map/all_to_all | solution.py:104
  769.3 226.1 %all-gather.12.cloned.1.call-done = f32[8192,1024]{1,0:T(8,128)} async-done(((f32[2048,1024]{1,0:T(8,128)}), f32[8192,1024]{1,0:T(8,128)}) %all-gather.12.cloned.1.call-update) | async-done | bytes 33554448 | tf_op jit(solution)/shard_map/all_gather | solution.py:170
  995.4 16.5 %reduce_sum.98 = f32[2048,1024]{1,0:T(8,128)} reduce(f32[4,2048,1024]{2,1,0:T(8,128)} %bitcast.108, f32[]{:T(128)} %constant.79.clone.1), dimensions={0}, to_apply=%region_12.13 | reduce | flops 6291456 | bytes 41943044 | tf_op jit(solution)/shard_map/reduce_sum | solution.py:170
  1011.9 5.5 convert_reduce_fusion.1
  1019.4 5.4 fusion.65
  1024.8 23.0 %fusion.30 = f32[2048,1024]{1,0:T(8,128)} fusion(f32[2048,656]{0,1:T(8,128)} %fusion.65, bf16[128,8,656]{2,1,0:T(8,128)(2,1)} %gather_fusion.7, bf16[128,8,656]{2,1,0:T(8,128)(2,1)S(1)} %copy-done.12, bf16[2048,1024]{1,0:T(8,128)(2,1)} %copy-done.5, f32[1024]{0:T(1024)S(1)} %copy-done.25, f32[2048]{0:T(1024)S(1)} %get-tuple-element.173, ...), kind=kOutput, calls=%fused_computation.64 | convolution fusion | flops 5602082816 | bytes 20664320 | tf_op jit(solution)/shard_map/dot_general | solution.py:177
  1048.5 80.5 %reduce-scatter.2.cloned.1.call-done = f32[2048,256]{1,0:T(8,128)} async-done(((f32[2048,1024]{1,0:T(8,128)}), f32[2048,256]{1,0:T(8,128)}) %reduce-scatter.2.cloned.1.call-update) | async-done | bytes 2097168 | tf_op jit(solution)/shard_map/reduce_scatter | solution.py:180
  1132.6 143.3 %all-reduce.2.cloned.1.call-done = f32[64,1024]{1,0:T(8,128)} async-done(((f32[64,1024]{1,0:T(8,128)}), f32[64,1024]{1,0:T(8,128)}) %all-reduce.2.cloned.1.call-update) | async-done | bytes 262160 | tf_op jit(solution)/shard_map/psum | solution.py:190
  1279.2 63.4 %pmax.7 = f32[64]{0:T(128)} all-reduce(f32[64]{0:T(128)S(1)} %convolution_reduce_fusion), channel_id=1, replica_groups=mesh['req'=32,'tp'=4] {'req','tp'}, use_global_device_ids=true, to_apply=%region_20.21 | all-reduce | flops 64 | bytes 512 | tf_op jit(solution)/shard_map/pmax | solution.py:205
  (297 shorter events, 222.6 us)
Async XLA Ops:
  7.2 1270.3 %copy-start = (f32[4,1024]{1,0:T(4,128)S(1)}, f32[4,1024]{1,0:T(4,128)}, u32[]{:S(2)}) copy-start(f32[4,1024]{1,0:T(4,128)} %param.33) | copy-start | bytes 49156
  7.2 113.7 %copy-start.1 = (s32[128]{0:T(128)S(1)}, s32[128]{0:T(128)}, u32[]{:S(2)}) copy-start(s32[128]{0:T(128)} %param.22) | copy-start | bytes 1540
  7.2 115.9 %copy-start.15 = (f32[8,1024]{1,0:T(8,128)S(1)}, f32[8,1024]{1,0:T(8,128)}, u32[]{:S(2)}) copy-start(f32[8,1024]{1,0:T(8,128)} %param.23) | copy-start | bytes 98308
  7.2 192.6 %copy-start.16 = (f32[8,1024]{1,0:T(8,128)S(1)}, f32[8,1024]{1,0:T(8,128)}, u32[]{:S(2)}) copy-start(f32[8,1024]{1,0:T(8,128)} %param.25) | copy-start | bytes 98308
  7.2 271.1 %copy-start.21 = (f32[1024]{0:T(1024)S(1)}, f32[1024]{0:T(1024)}, u32[]{:S(2)}) copy-start(f32[1024]{0:T(1024)} %param.31) | copy-start | bytes 12292
  7.2 662.4 %all-gather.6.cloned.1.call-start = ((), (), s32[]{:S(2)}) async-start(), calls=%async_computation.8 | async-start | bytes 1419264 | tf_op jit(solution)/shard_map/all_gather | solution.py:93
  95.9 189.0 %all-to-all-start.1 = ((bf16[256,4,256]{0,2,1:T(8,128)(2,1)}), bf16[256,4,256]{0,2,1:T(8,128)(2,1)S(1)}, u32[]{:S(2)}, u32[]{:S(2)}) async-start(bf16[256,4,256]{0,2,1:T(8,128)(2,1)} %bitcast.18), calls=%async_computation.1 | async-start | bytes 1048576 | tf_op jit(solution)/shard_map/all_to_all | solution.py:99
  114.4 562.1 %all-gather.8.cloned.1.call-start = ((), (), s32[]{:S(2)}) async-start(), calls=%async_computation.9 | async-start | bytes 1419264 | tf_op jit(solution)/shard_map/all_gather | solution.py:94
  117.4 363.3 %copy-start.19 = (s32[64]{0:T(128)}, s32[64]{0:T(128)S(1)}, u32[]{:S(2)}) copy-start(s32[64]{0:T(128)S(1)} %get-tuple-element.126) | copy-start | bytes 772
  123.1 365.0 %copy-start.18 = (s32[1024]{0:T(1024)}, s32[1024]{0:T(1024)S(1)}, u32[]{:S(2)}) copy-start(s32[1024]{0:T(1024)S(1)} %pad_clamp_fusion.1) | copy-start | bytes 12292
  278.3 6.4 copy-start.22
  284.9 39.4 %all-to-all-start = ((bf16[256,4,256]{0,2,1:T(8,128)(2,1)}), bf16[256,4,256]{0,2,1:T(8,128)(2,1)S(1)}, u32[]{:S(2)}, u32[]{:S(2)}) async-start(bf16[256,4,256]{0,2,1:T(8,128)(2,1)} %bitcast.7), calls=%async_computation | async-start | bytes 1048576 | tf_op jit(solution)/shard_map/all_to_all | solution.py:98
  324.3 13.3 all-to-all-start.2
  338.4 8.0 copy-start.17
  341.9 137.8 %copy-start.14 = (f32[8,2624]{1,0:T(8,128)S(1)}, f32[8,2624]{1,0:T(8,128)}, u32[]{:S(2)}) copy-start(f32[8,2624]{1,0:T(8,128)} %param.29) | copy-start | bytes 251908
  342.1 147.4 %copy-start.9 = (bf16[2,2048,256]{2,1,0:T(8,128)(2,1)}, bf16[2,2048,256]{2,1,0:T(8,128)(2,1)S(1)}, u32[]{:S(2)}) copy-start(bf16[2,2048,256]{2,1,0:T(8,128)(2,1)S(1)} %pad_maximum_fusion.1) | copy-start | bytes 6291460
  342.1 147.4 %collective-permute-start = (bf16[2,2048,256]{2,1,0:T(8,128)(2,1)S(1)}, bf16[2,2048,256]{2,1,0:T(8,128)(2,1)}, u32[]{:S(2)}, u32[]{:S(2)}) collective-permute-start(bf16[2,2048,256]{2,1,0:T(8,128)(2,1)S(1)} %pad_maximum_fusion.1), channel_id=1, source_target_pairs={{0,4},{4,8},{8,12},{12,16},{16,20},{20,24},{24,28},{28,32},{32,36}... | collective-permute-start | bytes 6291464 | tf_op jit(solution)/shard_map/ppermute | solution.py:17
  345.2 144.4 %collective-permute-start.1 = (bf16[2,2048,256]{2,1,0:T(8,128)(2,1)S(1)}, bf16[2,2048,256]{2,1,0:T(8,128)(2,1)}, u32[]{:S(2)}, u32[]{:S(2)}) collective-permute-start(bf16[2,2048,256]{2,1,0:T(8,128)(2,1)S(1)} %pad_maximum_fusion.1), channel_id=1, source_target_pairs={{4,0},{8,4},{12,8},{16,12},{20,16},{24,20},{28,24},{32,28},{36,32}... | collective-permute-start | bytes 6291464 | tf_op jit(solution)/shard_map/ppermute | solution.py:20
  462.4 25.5 %all-to-all-start.3 = ((bf16[256,4,256]{0,2,1:T(8,128)(2,1)}), bf16[256,4,256]{0,2,1:T(8,128)(2,1)S(1)}, u32[]{:S(2)}, u32[]{:S(2)}) async-start(bf16[256,4,256]{0,2,1:T(8,128)(2,1)} %bitcast.36), calls=%async_computation.3 | async-start | bytes 1048576 | tf_op jit(solution)/shard_map/all_to_all | solution.py:101
  479.7 218.0 %all-gather.10.cloned.1.call-start = ((), (), s32[]{:S(2)}) async-start(), calls=%async_computation.10 | async-start | bytes 1419264 | tf_op jit(solution)/shard_map/all_gather | solution.py:95
  480.5 514.9 %all-gather.12.cloned.1.call-start = ((), (), s32[]{:S(2)}) async-start(), calls=%async_computation.13 | async-start | bytes 41943040 | tf_op jit(solution)/shard_map/all_gather | solution.py:170
  672.1 21.1 %all-to-all-start.4 = ((bf16[256,4,656]{0,2,1:T(8,128)(2,1)}), bf16[256,4,656]{0,2,1:T(8,128)(2,1)S(1)}, u32[]{:S(2)}, u32[]{:S(2)}) async-start(bf16[256,4,656]{0,2,1:T(8,128)(2,1)} %bitcast.41), calls=%async_computation.4 | async-start | bytes 2686976 | tf_op jit(solution)/shard_map/all_to_all | solution.py:102
  693.2 35.7 %all-to-all-start.5 = ((bf16[256,4,656]{0,2,1:T(8,128)(2,1)}), bf16[256,4,656]{0,2,1:T(8,128)(2,1)S(1)}, u32[]{:S(2)}, u32[]{:S(2)}) async-start(bf16[256,4,656]{0,2,1:T(8,128)(2,1)} %bitcast.118), calls=%async_computation.5 | async-start | bytes 2686976 | tf_op jit(solution)/shard_map/all_to_all | solution.py:103
  729.0 5.5 copy-start.6
  729.0 36.8 %all-to-all-start.6 = ((bf16[256,4,656]{0,2,1:T(8,128)(2,1)}), bf16[256,4,656]{0,2,1:T(8,128)(2,1)}, u32[]{:S(2)}, u32[]{:S(2)}) async-start(bf16[256,4,656]{0,2,1:T(8,128)(2,1)} %bitcast.117), calls=%async_computation.6 | async-start | bytes 2686976 | tf_op jit(solution)/shard_map/all_to_all | solution.py:104
  734.2 394.8 %reduce-scatter.2.cloned.1.call-start = ((), (), s32[]{:S(2)}) async-start(), calls=%async_computation.11 | async-start | bytes 10485760 | tf_op jit(solution)/shard_map/reduce_scatter | solution.py:180
  1011.9 7.5 copy-start.25
  1019.4 5.4 copy-start.12
  1047.8 229.7 %copy-start.24 = (s32[64]{0:T(128)S(1)}, s32[64]{0:T(128)}, u32[]{:S(2)}) copy-start(s32[64]{0:T(128)} %param.21) | copy-start | bytes 772
  1047.8 231.0 %copy-start.11 = (f32[384,1024]{1,0:T(8,128)S(1)}, f32[384,1024]{1,0:T(8,128)}, u32[]{:S(2)}) copy-start(f32[384,1024]{1,0:T(8,128)} %param.30) | copy-start | bytes 4718596
  1047.8 228.1 %all-reduce.2.cloned.1.call-start = ((), (), s32[]{:S(2)}) async-start(), calls=%async_computation.12 | async-start | bytes 524288 | tf_op jit(solution)/shard_map/psum | solution.py:190
  1131.1 211.5 %copy-start.10 = (bf16[2048,256]{1,0:T(8,128)(2,1)}, bf16[2048,256]{1,0:T(8,128)(2,1)S(1)}, u32[]{:S(2)}) copy-start(bf16[2048,256]{1,0:T(8,128)(2,1)S(1)} %add_convert_fusion) | copy-start | bytes 3145732
  (24 other events, 50.7 us)
Sparse Core Ops, SparseCore 0:
  11.1 70.7 all-gather.5
  118.3 62.2 all-gather.7
  483.6 72.6 all-gather.9
  669.7 325.6 all-gather.11
  1047.9 81.0 reduce-scatter.1
  1133.6 142.2 all-reduce.1
